TPU v7x, 512 devices: a whole 4x8x8 slice. The times are simulated.
512 devices in a mesh: dp: 8 (over z), expert: 64 (over x, y, core).
Axes of the slice: x: 4, y: 8, z: 8, core: 2. Of those that a mesh axis runs over, the one named last changes fastest.
Arguments:
- tokens: bfloat16 [65536, 1024], P(('dp', 'expert')), may hold values from -6 to 6
- d_output: bfloat16 [65536, 1024], P(('dp', 'expert')), may hold values from -6 to 6
- combine: float32 [65536, 8], P(('dp', 'expert')), may hold values from 0.05 to 1
- routes: int32 [65536, 8], P(('dp', 'expert')), may hold values from 0 to 63, all different within a row; in each aligned block of 128 rows (0 to 127, 128 to 255, ...) at most 18 rows name the same one
- gate_weight: bfloat16 [64, 1024, 384], P('expert', 'dp'), may hold values from -0.1875 to 0.1875
- up_weight: bfloat16 [64, 1024, 384], P('expert', 'dp'), may hold values from -0.1875 to 0.1875
- down_weight: bfloat16 [64, 384, 1024], P('expert', None, 'dp'), may hold values from -0.3125 to 0.3125
Outputs:
- d_tokens: bfloat16 [65536, 1024], P(('dp', 'expert'))
- d_gate_weight: float32 [64, 1024, 384], P('expert', 'dp')
- d_up_weight: float32 [64, 1024, 384], P('expert', 'dp')
- d_down_weight: float32 [64, 384, 1024], P('expert', None, 'dp')
Inputs may be any that keep to these rules, and one draw needn't show every extreme that they name: `routes`: among the 128 tokens of one device, each expert id is named by at most 18 rows; some expert is named by exactly 18 rows on some device. The ids of one token differ.
All inputs are finite; a program needn't handle non-finite values.
Results may differ from a plain program's by a relative error of at most 0.015.
Values may be sent and summed in bfloat16 or wider, within the bound.
A program may use at most 64 MiB of HBM per device.

v0:
```python
import jax
import jax.numpy as jnp
from jax import lax
from jax.sharding import PartitionSpec as P


def route_slots(routes, experts):
    matches = (routes[:, :, None] == jnp.arange(experts, dtype=jnp.int32)[None, None, :]).astype(
        jnp.int32
    )
    per_token = jnp.sum(matches, axis=1)
    earlier = jnp.cumsum(per_token, axis=0) - per_token
    return jnp.sum(matches * earlier[:, None, :], axis=2)


def row_work(row_inputs, row_grads, gate_up, down_matrix):
    hidden_units = down_matrix.shape[0]
    preact = jnp.dot(row_inputs, gate_up, preferred_element_type=jnp.float32)
    gate_pre = preact[:, :hidden_units]
    up_pre = preact[:, hidden_units:]
    gate_sigmoid = jax.nn.sigmoid(gate_pre)
    hidden = (gate_pre * gate_sigmoid * up_pre).astype(jnp.bfloat16)
    d_hidden = jnp.dot(row_grads, down_matrix.T, preferred_element_type=jnp.float32)
    d_gate_pre = d_hidden * up_pre * gate_sigmoid * (1.0 + gate_pre * (1.0 - gate_sigmoid))
    d_up_pre = d_hidden * gate_pre * gate_sigmoid
    d_preact = jnp.concatenate([d_gate_pre, d_up_pre], axis=1).astype(jnp.bfloat16)
    d_rows = jnp.dot(d_preact, gate_up.T, preferred_element_type=jnp.float32).astype(jnp.bfloat16)
    return (d_rows, hidden, d_preact)


def body(tokens, d_output, combine, routes, gate_weight, up_weight, down_weight):
    experts = lax.axis_size("expert")
    tok_count = tokens.shape[0]
    model_width = tokens.shape[1]
    top_count = routes.shape[1]
    capacity = max(2, (9 * tok_count * top_count + 8 * experts - 1) // (8 * experts))
    slot_count = experts * capacity
    slot_index = route_slots(routes, experts)
    position = (routes * capacity + slot_index).reshape(-1)
    spread_inputs = jnp.repeat(tokens, top_count, axis=0)
    scaled = (
        (combine[:, :, None] * d_output[:, None, :].astype(jnp.float32))
        .astype(jnp.bfloat16)
        .reshape(-1, model_width)
    )
    send_inputs = (
        jnp.zeros((slot_count, model_width), jnp.bfloat16)
        .at[position]
        .set(spread_inputs)
        .reshape(experts, capacity, model_width)
    )
    send_grads = (
        jnp.zeros((slot_count, model_width), jnp.bfloat16)
        .at[position]
        .set(scaled)
        .reshape(experts, capacity, model_width)
    )
    whole_gate, whole_up, whole_down = (
        lax.all_gather(gate_weight, "dp", axis=1, tiled=True),
        lax.all_gather(up_weight, "dp", axis=1, tiled=True),
        lax.all_gather(down_weight, "dp", axis=2, tiled=True),
    )
    gate_up = jnp.concatenate([whole_gate[0], whole_up[0]], axis=1)
    down_matrix = whole_down[0]
    hidden_units = down_matrix.shape[0]
    recv_inputs, recv_grads = (
        lax.all_to_all(send_inputs, "expert", split_axis=0, concat_axis=0, tiled=True),
        lax.all_to_all(send_grads, "expert", split_axis=0, concat_axis=0, tiled=True),
    )
    flat_inputs = recv_inputs.reshape(-1, model_width)
    flat_grads = recv_grads.reshape(-1, model_width)
    d_rows, hidden, d_preact = row_work(flat_inputs, flat_grads, gate_up, down_matrix)
    returned = lax.all_to_all(
        d_rows.reshape(experts, capacity, model_width),
        "expert",
        split_axis=0,
        concat_axis=0,
        tiled=True,
    )
    route_rows = returned.reshape(-1, model_width)[position].reshape(
        tok_count, top_count, model_width
    )
    d_tokens = jnp.sum(route_rows.astype(jnp.float32), axis=1).astype(jnp.bfloat16)
    gate_up_grad = jnp.dot(flat_inputs.T, d_preact, preferred_element_type=jnp.float32)
    down_grad = jnp.dot(flat_grads.T, hidden, preferred_element_type=jnp.float32)
    stacked = jnp.concatenate([gate_up_grad, down_grad], axis=1)
    summed = lax.psum_scatter(
        stacked.astype(jnp.bfloat16), "dp", scatter_dimension=0, tiled=True
    ).astype(jnp.float32)
    d_gate_weight = summed[:, :hidden_units][None]
    d_up_weight = summed[:, hidden_units : 2 * hidden_units][None]
    d_down_weight = summed[:, 2 * hidden_units :].T[None]
    return (d_tokens, d_gate_weight, d_up_weight, d_down_weight)


def solution(mesh):
    placed = (
        P(("dp", "expert"), None),
        P(("dp", "expert"), None),
        P(("dp", "expert"), None),
        P(("dp", "expert"), None),
        P("expert", "dp", None),
        P("expert", "dp", None),
        P("expert", None, "dp"),
    )
    return jax.shard_map(
        body,
        mesh=mesh,
        in_specs=placed,
        out_specs=(
            P(("dp", "expert"), None),
            P("expert", "dp", None),
            P("expert", "dp", None),
            P("expert", None, "dp"),
        ),
        check_vma=False,
    )
```

profile of v0, /device:TPU:1, one launch (start us, length us, event | category | flops | bytes accessed | tf_op | source)
XLA Modules:
  0.0 330.5 jit_solution(18078661174576874476)
XLA Ops:
  7.2 0.0 copy-start
  7.2 0.8 convert_reduce_fusion
  7.9 0.1 copy.24
  8.0 0.2 reduce_window_sum.11
  8.2 0.1 copy.26
  8.3 0.7 select_reduce_fusion
  9.0 0.7 multiply_add_fusion
  9.7 0.1 copy.27
  9.8 0.1 reshape.80
  10.0 0.0 copy-done
  10.0 6.0 %scatter_custom_fusion.1 = bf16[1152,1024]{1,0:T(8,128)(2,1)S(1)} fusion(s32[1024]{0:T(1024)S(1)} %bitcast.37, bf16[]{:T(256)} %constant.5.clone.1, bf16[128,1024]{1,0:T(8,128)(2,1)S(1)} %copy-done), kind=kCustom, calls=%fused_computation.9 | custom fusion | bytes 2621442 | tf_op jit(solution)/shard_map/scatter | solution.py:49
  16.0 2.4 reshape.84
  18.4 0.0 copy-start.6
  18.4 11.8 %all-to-all-start.1 = ((bf16[64,18,1024]{2,1,0:T(8,128)(2,1)}), bf16[64,18,1024]{2,1,0:T(8,128)(2,1)S(1)}, u32[]{:S(2)}, u32[]{:S(2)}) async-start(bf16[64,18,1024]{2,1,0:T(8,128)(2,1)} %reshape.84), calls=%async_computation.1 | async-start | bytes 6291456 | tf_op jit(solution)/shard_map/all_to_all | solution.py:67
  30.2 0.0 copy-done.6
  30.2 0.1 copy.28
  30.3 0.1 mul.60
  30.4 1.8 convert_element_type.25
  32.2 7.7 %scatter_custom_fusion = bf16[1152,1024]{1,0:T(8,128)(2,1)} fusion(s32[1024]{0:T(1024)S(1)} %bitcast.38, f32[128,1024]{1,0:T(8,128)} %convert_element_type.25, f32[1024]{0:T(1024)S(1)} %mul.60, bf16[]{:T(256)} %constant.5.clone.1), kind=kCustom, calls=%fused_computation.7 | custom fusion | flops 2097152 | bytes 2887682 | tf_op jit(solution)/shard_map/scatter | solution.py:55
  39.9 4.3 %reshape.81 = bf16[64,18,1024]{2,1,0:T(8,128)(2,1)} reshape(bf16[1152,1024]{1,0:T(8,128)(2,1)} %scatter_custom_fusion) | data formatting | bytes 4718592 | tf_op jit(solution)/shard_map/reshape | solution.py:56
  44.2 0.0 copy-start.5
  44.2 59.5 %all-to-all-done.1 = bf16[64,18,1024]{2,1,0:T(8,128)(2,1)S(1)} async-done(((bf16[64,18,1024]{2,1,0:T(8,128)(2,1)}), bf16[64,18,1024]{2,1,0:T(8,128)(2,1)S(1)}, u32[]{:S(2)}, u32[]{:S(2)}) %all-to-all-start.1) | async-done | bytes 2359328 | tf_op jit(solution)/shard_map/all_to_all | solution.py:67
  103.7 6.2 %all-to-all-start = ((bf16[64,18,1024]{2,1,0:T(8,128)(2,1)}), bf16[64,18,1024]{2,1,0:T(8,128)(2,1)}, u32[]{:S(2)}, u32[]{:S(2)}) async-start(bf16[64,18,1024]{2,1,0:T(8,128)(2,1)} %reshape.81), calls=%async_computation | async-start | bytes 6291456 | tf_op jit(solution)/shard_map/all_to_all | solution.py:68
  109.9 0.0 copy-done.5
  109.9 30.3 %all_gather.10 = bf16[1,1024,384]{2,1,0:T(8,128)(2,1)} all-gather(bf16[1,128,384]{2,1,0:T(8,128)(2,1)S(1)} %copy-done.5), channel_id=1, replica_groups=mesh['dp'=8,'expert'=64] {'dp'}, dimensions={1}, use_global_device_ids=true | all-gather | bytes 884736 | tf_op jit(solution)/shard_map/all_gather | solution.py:59
  140.2 24.1 %all_gather.11 = bf16[1,1024,384]{2,1,0:T(8,128)(2,1)} all-gather(bf16[1,128,384]{2,1,0:T(8,128)(2,1)} %param.12), channel_id=1, replica_groups=mesh['dp'=8,'expert'=64] {'dp'}, dimensions={1}, use_global_device_ids=true | all-gather | bytes 884736 | tf_op jit(solution)/shard_map/all_gather | solution.py:60
  164.3 22.5 %all_gather.9 = bf16[1,384,1024]{2,1,0:T(8,128)(2,1)} all-gather(bf16[1,384,128]{2,1,0:T(8,128)(2,1)} %param.13), channel_id=1, replica_groups=mesh['dp'=8,'expert'=64] {'dp'}, dimensions={2}, use_global_device_ids=true | all-gather | bytes 884736 | tf_op jit(solution)/shard_map/all_gather | solution.py:61
  186.8 2.2 reshape.85
  189.0 6.1 %fusion.10 = f32[1152,768]{0,1:T(8,128)} fusion(bf16[1152,1024]{1,0:T(8,128)(2,1)} %reshape.85, bf16[1024,384]{1,0:T(8,128)(2,1)} %bitcast.35, bf16[1024,384]{1,0:T(8,128)(2,1)} %bitcast.33), kind=kOutput, calls=%fused_computation.24 | convolution fusion | flops 1815085056 | bytes 7471104 | tf_op jit(solution)/shard_map/dot_general | solution.py:18
  195.1 0.0 all-to-all-done
  195.1 2.9 reshape.82
  198.1 0.0 copy-start.4
  198.1 0.0 copy-start.7
  198.1 3.4 %convolution_convert_fusion.2 = bf16[1024,384]{0,1:T(8,128)(2,1)S(1)} fusion(bf16[1152,1024]{1,0:T(8,128)(2,1)S(1)} %reshape.82, f32[1152,768]{0,1:T(8,128)} %fusion.10), kind=kOutput, calls=%fused_computation.20 | convolution fusion | flops 909017088 | bytes 6684672 | tf_op jit(solution)/shard_map/dot_general | solution.py:85
  201.5 0.0 copy-done.4
  201.5 0.0 copy-done.7
  201.5 0.0 copy-start.1
  201.5 1.6 multiply_convert_fusion.2
  203.1 0.0 copy-done.1
  203.1 0.0 copy-start.2
  203.1 0.0 copy-start.3
  203.2 3.3 %convolution_convert_fusion.1 = bf16[1024,768]{0,1:T(8,128)(2,1)} fusion(bf16[1152,1024]{1,0:T(8,128)(2,1)S(1)} %copy-done.1, bf16[1152,384]{0,1:T(8,128)(2,1)S(1)} %get-tuple-element.21, bf16[1152,384]{0,1:T(8,128)(2,1)S(1)} %get-tuple-element.20), kind=kOutput, calls=%fused_computation.18 | convolution fusion | flops 1816264704 | bytes 5701632 | tf_op jit(solution)/shard_map/dot_general | solution.py:84
  206.5 0.0 copy-done.2
  206.5 0.0 copy-done.3
  206.5 2.1 convolution_convert_fusion
  208.6 2.5 reshape.86
  211.0 23.6 %all-to-all-start.2 = ((bf16[64,18,1024]{2,1,0:T(8,128)(2,1)}), bf16[64,18,1024]{2,1,0:T(8,128)(2,1)}, u32[]{:S(2)}, u32[]{:S(2)}) async-start(bf16[64,18,1024]{2,1,0:T(8,128)(2,1)} %reshape.86), calls=%async_computation.2 | async-start | bytes 6291456 | tf_op jit(solution)/shard_map/all_to_all | solution.py:73
  234.7 0.3 reduce-scatter.4.cloned.1.call-start
  234.9 1.6 pad_maximum_fusion
  236.5 2.5 copy.31
  239.1 0.0 reduce-scatter.4.cloned.1.call-update
  239.1 69.0 %all-to-all-done.2 = bf16[64,18,1024]{2,1,0:T(8,128)(2,1)} async-done(((bf16[64,18,1024]{2,1,0:T(8,128)(2,1)}), bf16[64,18,1024]{2,1,0:T(8,128)(2,1)}, u32[]{:S(2)}, u32[]{:S(2)}) %all-to-all-start.2) | async-done | bytes 2359328 | tf_op jit(solution)/shard_map/all_to_all | solution.py:73
  308.1 2.9 reshape.87
  311.0 5.4 %gather_fusion = bf16[1024,1024]{1,0:T(8,128)(2,1)} fusion(bf16[1152,1024]{1,0:T(8,128)(2,1)S(1)} %reshape.87, s32[1024]{0:T(1024)S(1)} %broadcast_clamp_fusion), kind=kCustom, calls=%fused_computation | custom fusion | bytes 4198400 | tf_op jit(solution)/shard_map/gather | solution.py:80
  316.4 3.7 %bitcast_reduce_fusion = bf16[128,1024]{1,0:T(8,128)(2,1)} fusion(bf16[1024,1024]{1,0:T(8,128)(2,1)} %gather_fusion), kind=kLoop, calls=%fused_computation.8 | loop fusion | flops 917504 | bytes 2359296 | tf_op jit(solution)/shard_map/reduce_sum | solution.py:83
  320.1 0.0 reduce-scatter.4.cloned.1.call-done
  320.1 1.2 copy.32
  321.3 0.7 slice_bitcast_fusion
  322.1 0.8 copy.30
  322.9 0.8 copy.29
  (4 shorter events, 0.1 us)
Async XLA Ops:
  7.2 2.8 copy-start
  18.4 11.8 %copy-start.6 = (f32[128,8]{0,1:T(8,128)S(1)}, f32[128,8]{0,1:T(8,128)}, u32[]{:S(2)}) copy-start(f32[128,8]{0,1:T(8,128)} %param.9) | copy-start | bytes 12292
  18.4 85.3 %all-to-all-start.1 = ((bf16[64,18,1024]{2,1,0:T(8,128)(2,1)}), bf16[64,18,1024]{2,1,0:T(8,128)(2,1)S(1)}, u32[]{:S(2)}, u32[]{:S(2)}) async-start(bf16[64,18,1024]{2,1,0:T(8,128)(2,1)} %reshape.84), calls=%async_computation.1 | async-start | bytes 6291456 | tf_op jit(solution)/shard_map/all_to_all | solution.py:67
  44.2 65.8 %copy-start.5 = (bf16[1,128,384]{2,1,0:T(8,128)(2,1)S(1)}, bf16[1,128,384]{2,1,0:T(8,128)(2,1)}, u32[]{:S(2)}) copy-start(bf16[1,128,384]{2,1,0:T(8,128)(2,1)} %param.11) | copy-start | bytes 294916
  103.7 91.5 %all-to-all-start = ((bf16[64,18,1024]{2,1,0:T(8,128)(2,1)}), bf16[64,18,1024]{2,1,0:T(8,128)(2,1)}, u32[]{:S(2)}, u32[]{:S(2)}) async-start(bf16[64,18,1024]{2,1,0:T(8,128)(2,1)} %reshape.81), calls=%async_computation | async-start | bytes 6291456 | tf_op jit(solution)/shard_map/all_to_all | solution.py:68
  198.1 3.4 %copy-start.4 = (bf16[1,384,1024]{2,1,0:T(8,128)(2,1)S(1)}, bf16[1,384,1024]{2,1,0:T(8,128)(2,1)}, u32[]{:S(2)}) copy-start(bf16[1,384,1024]{2,1,0:T(8,128)(2,1)} %all_gather.9) | copy-start | bytes 2359300
  198.1 3.4 %copy-start.7 = (f32[1152,768]{0,1:T(8,128)S(1)}, f32[1152,768]{0,1:T(8,128)}, u32[]{:S(2)}) copy-start(f32[1152,768]{0,1:T(8,128)} %fusion.10) | copy-start | bytes 10616836
  201.5 1.7 copy-start.1
  203.1 3.3 %copy-start.2 = (bf16[1,1024,384]{2,1,0:T(8,128)(2,1)S(1)}, bf16[1,1024,384]{2,1,0:T(8,128)(2,1)}, u32[]{:S(2)}) copy-start(bf16[1,1024,384]{2,1,0:T(8,128)(2,1)} %all_gather.10) | copy-start | bytes 2359300
  203.1 3.3 %copy-start.3 = (bf16[1,1024,384]{2,1,0:T(8,128)(2,1)S(1)}, bf16[1,1024,384]{2,1,0:T(8,128)(2,1)}, u32[]{:S(2)}) copy-start(bf16[1,1024,384]{2,1,0:T(8,128)(2,1)} %all_gather.11) | copy-start | bytes 2359300
  211.0 97.1 %all-to-all-start.2 = ((bf16[64,18,1024]{2,1,0:T(8,128)(2,1)}), bf16[64,18,1024]{2,1,0:T(8,128)(2,1)}, u32[]{:S(2)}, u32[]{:S(2)}) async-start(bf16[64,18,1024]{2,1,0:T(8,128)(2,1)} %reshape.86), calls=%async_computation.2 | async-start | bytes 6291456 | tf_op jit(solution)/shard_map/all_to_all | solution.py:73
  234.7 85.5 %reduce-scatter.4.cloned.1.call-start = ((), (), s32[]{:S(2)}) async-start(), calls=%async_computation.4 | async-start | bytes 2654208
Sparse Core Ops, SparseCore 0:
  239.2 41.3 reduce-scatter.3
where the time goes:
time: 331 us
  waiting for transfers between devices  129 us (39%)
  blocking collectives  76.9 us (23%)
  starting transfers between devices  41.9 us (13%)
  local copies, waits for them, and re-layouts  35.3 us (11%)
  other arithmetic  17.3 us (5%)
  matrix products  16.5 us (5%)
  between operations  14.2 us (4%)
    all_to_all x1, waiting for transfers between devices, body(): lax.all_to_all(d_rows.reshape(experts, capacity, model_width), 'expert',...  69 us
    all_to_all x1, waiting for transfers between devices, body(): lax.all_to_all(send_inputs, 'expert', split_axis=0, concat_axis=0, tiled=...  59.5 us
    all_gather x1, blocking collectives, body(): lax.all_gather(gate_weight, 'dp', axis=1, tiled=True)  30.3 us
    all_gather x1, blocking collectives, body(): lax.all_gather(up_weight, 'dp', axis=1, tiled=True)  24.1 us
    all_to_all x1, starting transfers between devices, body(): lax.all_to_all(d_rows.reshape(experts, capacity, model_width), 'expert',...  23.6 us
    all_gather x1, blocking collectives, body(): lax.all_gather(down_weight, 'dp', axis=2, tiled=True)  22.5 us
    all_to_all x1, starting transfers between devices, body(): lax.all_to_all(send_inputs, 'expert', split_axis=0, concat_axis=0, tiled=...  11.8 us
    scatter x1, other arithmetic, body(): send_grads = jnp.zeros((slot_count, model_width), jnp.bfloat16).at[positi...  7.71 us
  transfers between devices with their start and end apart: 4, of which 2 were waited for; matrix products, arithmetic and copies ran while one was open for 12% of the time, Pallas kernels for 0%

commit v1 on v0

--- a/solution.py
+++ b/solution.py
@@ -1,7 +1,36 @@
+import functools
 import jax
 import jax.numpy as jnp
 from jax import lax
 from jax.sharding import PartitionSpec as P
+
+
+def test_the_packet(block_here, axis_id):
+    r1 = lax.psum(1, axis_name=axis_id)
+    opened = lax.axis_index(axis_id)
+    x_new, parts_out, met_up = (r1, opened, block_here.shape[1])
+    bank = [to_i * x_new if idx == 1 else to_i for idx, to_i in enumerate(block_here.shape)]
+    mat_out = jnp.zeros(bank, block_here.dtype)
+    val = lax.dynamic_update_slice_in_dim(mat_out, block_here, parts_out * met_up, axis=1)
+    high = x_next = block_here
+    i0 = 1
+    while i0 < x_new // 2 + 1:
+        high = lax.ppermute(
+            high, axis_name=axis_id, perm=[(idx, (idx + 1) % x_new) for idx in range(x_new)]
+        )
+        val = lax.dynamic_update_slice_in_dim(val, high, (parts_out - i0) % x_new * met_up, axis=1)
+        if 2 * i0 < x_new:
+            x_next = lax.ppermute(
+                x_next, axis_name=axis_id, perm=[(idx, (idx - 1) % x_new) for idx in range(x_new)]
+            )
+            val = lax.dynamic_update_slice_in_dim(
+                val, x_next, (parts_out + i0) % x_new * met_up, axis=1
+            )
+        i0 = i0 + 1
+    return val
+
+
+reach_bars = functools.partial(test_the_packet, axis_id="dp")
 
 
 def route_slots(routes, experts):
@@ -56,7 +85,7 @@
         .reshape(experts, capacity, model_width)
     )
     whole_gate, whole_up, whole_down = (
-        lax.all_gather(gate_weight, "dp", axis=1, tiled=True),
+        reach_bars(gate_weight),
         lax.all_gather(up_weight, "dp", axis=1, tiled=True),
         lax.all_gather(down_weight, "dp", axis=2, tiled=True),
     )

time: 331 us -> 347 us (1.048)
  blocking collectives: 76.9 us -> 47.6 us
  starting transfers between devices: 41.9 us -> 67.5 us
  local copies, waits for them, and re-layouts: 35.3 us -> 44.6 us
  waiting for transfers between devices: 129 us -> 135 us
    all_gather x1 -> x0, blocking collectives: 30.3 us -> none  [body(): lax.all_gather(gate_weight, 'dp', axis=1, tiled=True)]
    ppermute x0 -> x7, starting transfers between devices: none -> 26.9 us  [the longest x3 19 us: test_the_packet(): lax.ppermute(x_next, axis_name=axis_id, perm=[(idx, (idx - 1) % x_new) fo...]
    dynamic_update_slice x0 -> x8, local copies, waits for them, and re-layouts: none -> 6.99 us  [the longest x4 3.51 us: test_the_packet(): lax.dynamic_update_slice_in_dim(val, high, (parts_out - i0) % x_new * met...]
    ppermute x0 -> x7, waiting for transfers between devices: none -> 6.49 us  [the longest x4 6.48 us: test_the_packet(): lax.ppermute(high, axis_name=axis_id, perm=[(idx, (idx + 1) % x_new) for...]
  transfers between devices with their start and end apart: 4 -> 11, of which waited for: 2 -> 4; matrix products, arithmetic and copies ran while one was open for 12% -> 13% of each run, Pallas kernels for 0% -> 0%
where the time goes in v1:
time: 347 us; the launch traced here: 346 us
  waiting for transfers between devices  135 us (39%)
  starting transfers between devices  67.5 us (19%)
  blocking collectives  47.6 us (14%)
  local copies, waits for them, and re-layouts  44.6 us (13%)
  matrix products  19.4 us (6%)
  other arithmetic  17.3 us (5%)
  between operations  14.3 us (4%)
    all_to_all x1, waiting for transfers between devices, body(): lax.all_to_all(d_rows.reshape(experts, capacity, model_width), 'expert',...  68.9 us
    all_to_all x1, waiting for transfers between devices, body(): lax.all_to_all(send_inputs, 'expert', split_axis=0, concat_axis=0, tiled=...  59.5 us
    all_gather x1, blocking collectives, body(): lax.all_gather(up_weight, 'dp', axis=1, tiled=True)  24.6 us
    all_gather x1, blocking collectives, body(): lax.all_gather(down_weight, 'dp', axis=2, tiled=True)  23 us
    all_to_all x1, starting transfers between devices, body(): lax.all_to_all(d_rows.reshape(experts, capacity, model_width), 'expert',...  22.3 us
    ppermute x3, starting transfers between devices, test_the_packet(): lax.ppermute(x_next, axis_name=axis_id, perm=[(idx, (idx - 1) % x_new) fo...  19 us
    all_to_all x1, starting transfers between devices, body(): lax.all_to_all(send_inputs, 'expert', split_axis=0, concat_axis=0, tiled=...  11.8 us
    ppermute x4, starting transfers between devices, test_the_packet(): lax.ppermute(high, axis_name=axis_id, perm=[(idx, (idx + 1) % x_new) for...  7.85 us
  transfers between devices with their start and end apart: 11, of which 4 were waited for; matrix products, arithmetic and copies ran while one was open for 13% of the time, Pallas kernels for 0%

profile of v1, /device:TPU:1, one launch (start us, length us, event | category | flops | bytes accessed | tf_op | source)
XLA Modules:
  0.0 345.6 jit_solution(15229145057112974437)
XLA Ops:
  7.2 0.0 copy-start
  7.2 0.8 convert_reduce_fusion
  7.9 0.1 copy.24
  8.0 0.2 reduce_window_sum.11
  8.2 0.1 copy.26
  8.3 0.7 select_reduce_fusion
  9.0 0.7 multiply_add_fusion
  9.7 0.1 copy.27
  9.8 0.1 reshape.96
  10.0 6.0 %scatter_custom_fusion.1 = bf16[1152,1024]{1,0:T(8,128)(2,1)S(1)} fusion(s32[1024]{0:T(1024)S(1)} %bitcast.50, bf16[]{:T(256)} %constant.69.clone.1, bf16[128,1024]{1,0:T(8,128)(2,1)S(1)} %copy-done), kind=kCustom, calls=%fused_computation.9 | custom fusion | bytes 2621442 | tf_op jit(solution)/shard_map/scatter | solution.py:78
  16.0 2.4 reshape.100
  18.4 11.8 %all-to-all-start.1 = ((bf16[64,18,1024]{2,1,0:T(8,128)(2,1)}), bf16[64,18,1024]{2,1,0:T(8,128)(2,1)S(1)}, u32[]{:S(2)}, u32[]{:S(2)}) async-start(bf16[64,18,1024]{2,1,0:T(8,128)(2,1)} %reshape.100), calls=%async_computation.1 | async-start | bytes 6291456 | tf_op jit(solution)/shard_map/all_to_all | solution.py:96
  30.2 0.1 copy.28
  30.3 0.1 mul.84
  30.4 1.8 convert_element_type.25
  32.2 7.7 %scatter_custom_fusion = bf16[1152,1024]{1,0:T(8,128)(2,1)} fusion(s32[1024]{0:T(1024)S(1)} %bitcast.51, f32[128,1024]{1,0:T(8,128)} %convert_element_type.25, f32[1024]{0:T(1024)S(1)} %mul.84, bf16[]{:T(256)} %constant.69.clone.1), kind=kCustom, calls=%fused_computation.7 | custom fusion | flops 2097152 | bytes 2887682 | tf_op jit(solution)/shard_map/scatter | solution.py:84
  39.9 4.3 %reshape.97 = bf16[64,18,1024]{2,1,0:T(8,128)(2,1)} reshape(bf16[1152,1024]{1,0:T(8,128)(2,1)} %scatter_custom_fusion) | data formatting | bytes 4718592 | tf_op jit(solution)/shard_map/reshape | solution.py:85
  44.2 59.5 %all-to-all-done.1 = bf16[64,18,1024]{2,1,0:T(8,128)(2,1)S(1)} async-done(((bf16[64,18,1024]{2,1,0:T(8,128)(2,1)}), bf16[64,18,1024]{2,1,0:T(8,128)(2,1)S(1)}, u32[]{:S(2)}, u32[]{:S(2)}) %all-to-all-start.1) | async-done | bytes 2359328 | tf_op jit(solution)/shard_map/all_to_all | solution.py:96
  103.6 6.2 %all-to-all-start = ((bf16[64,18,1024]{2,1,0:T(8,128)(2,1)}), bf16[64,18,1024]{2,1,0:T(8,128)(2,1)}, u32[]{:S(2)}, u32[]{:S(2)}) async-start(bf16[64,18,1024]{2,1,0:T(8,128)(2,1)} %reshape.97), calls=%async_computation | async-start | bytes 6291456 | tf_op jit(solution)/shard_map/all_to_all | solution.py:97
  109.9 10.7 %collective-permute-start.1 = (bf16[1,128,384]{2,1,0:T(8,128)(2,1)}, bf16[1,128,384]{2,1,0:T(8,128)(2,1)}, u32[]{:S(2)}, u32[]{:S(2)}) collective-permute-start(bf16[1,128,384]{2,1,0:T(8,128)(2,1)} %param.11), channel_id=1, source_target_pairs={{0,448},{64,0},{128,64},{192,128},{256,192},{320,256},{384,320},{4... | collective-permute-start | bytes 294920 | tf_op jit(solution)/shard_map/ppermute | solution.py:23
  120.6 1.9 collective-permute-start
  122.5 0.0 copy-start.6
  122.5 24.6 %all_gather.7 = bf16[1,1024,384]{2,1,0:T(8,128)(2,1)} all-gather(bf16[1,128,384]{2,1,0:T(8,128)(2,1)S(1)} %copy-done.5), channel_id=1, replica_groups=mesh['dp'=8,'expert'=64] {'dp'}, dimensions={1}, use_global_device_ids=true | all-gather | bytes 884736 | tf_op jit(solution)/shard_map/all_gather | solution.py:89
  147.1 23.0 %all_gather.6 = bf16[1,384,1024]{2,1,0:T(8,128)(2,1)} all-gather(bf16[1,384,128]{2,1,0:T(8,128)(2,1)} %param.13), channel_id=1, replica_groups=mesh['dp'=8,'expert'=64] {'dp'}, dimensions={2}, use_global_device_ids=true | all-gather | bytes 884736 | tf_op jit(solution)/shard_map/all_gather | solution.py:90
  170.1 1.0 squeeze.26
  171.1 0.6 bitcast_dynamic-update-slice_fusion.7
  171.7 3.8 %collective-permute-start.3 = (bf16[1,128,384]{2,1,0:T(8,128)(2,1)}, bf16[1,128,384]{2,1,0:T(8,128)(2,1)S(1)}, u32[]{:S(2)}, u32[]{:S(2)}) collective-permute-start(bf16[1,128,384]{2,1,0:T(8,128)(2,1)} %collective-permute-done.1), channel_id=1, source_target_pairs={{0,448},{64,0},{128,64},{192,128},{256,192},{320,256},{384,320},{4... | collective-permute-start | bytes 294920 | tf_op jit(solution)/shard_map/ppermute | solution.py:23
  175.5 0.0 collective-permute-done
  175.5 1.9 collective-permute-start.2
  177.4 1.5 bitcast_dynamic-update-slice_fusion.6
  179.0 1.5 bitcast_dynamic-update-slice_fusion.5
  180.5 4.6 %collective-permute-start.5 = (bf16[1,128,384]{2,1,0:T(8,128)(2,1)S(1)}, bf16[1,128,384]{2,1,0:T(8,128)(2,1)S(1)}, u32[]{:S(2)}, u32[]{:S(2)}) collective-permute-start(bf16[1,128,384]{2,1,0:T(8,128)(2,1)S(1)} %collective-permute-done.3), channel_id=1, source_target_pairs={{0,448},{64,0},{128,64},{192,128},{256,192},{320,256},{384,320},{4... | collective-permute-start | bytes 294920 | tf_op jit(solution)/shard_map/ppermute | solution.py:23
  185.1 0.0 collective-permute-done.2
  185.1 1.9 collective-permute-start.4
  187.0 0.6 bitcast_dynamic-update-slice_fusion.4
  187.7 0.7 bitcast_dynamic-update-slice_fusion.3
  188.3 3.3 collective-permute-done.4
  191.7 2.1 collective-permute-start.6
  193.8 0.7 bitcast_dynamic-update-slice_fusion.2
  194.4 0.7 bitcast_dynamic-update-slice_fusion.1
  195.1 3.1 collective-permute-done.6
  198.2 0.7 bitcast_dynamic-update-slice_fusion
  198.9 2.2 reshape.101
  201.1 6.1 %fusion.10 = f32[1152,768]{0,1:T(8,128)} fusion(bf16[1152,1024]{1,0:T(8,128)(2,1)} %reshape.101, bf16[1024,384]{1,0:T(8,128)(2,1)} %bitcast.48, bf16[1024,384]{1,0:T(8,128)(2,1)} %bitcast_dynamic-update-slice_fusion), kind=kOutput, calls=%fused_computation.24 | convolution fusion | flops 1815085056 | bytes 7471104 | tf_op jit(solution)/shard_map/dot_general | solution.py:47
  207.2 2.9 reshape.98
  210.2 1.4 copy-done.2
  211.6 3.4 convolution_convert_fusion.2
  215.0 3.4 multiply_convert_fusion.2
  218.4 3.3 convolution_convert_fusion.1
  221.8 3.2 convolution_convert_fusion
  225.0 2.4 reshape.102
  227.4 22.3 %all-to-all-start.2 = ((bf16[64,18,1024]{2,1,0:T(8,128)(2,1)}), bf16[64,18,1024]{2,1,0:T(8,128)(2,1)}, u32[]{:S(2)}, u32[]{:S(2)}) async-start(bf16[64,18,1024]{2,1,0:T(8,128)(2,1)} %reshape.102), calls=%async_computation.2 | async-start | bytes 6291456 | tf_op jit(solution)/shard_map/all_to_all | solution.py:102
  249.7 0.3 reduce-scatter.4.cloned.1.call-start
  250.0 1.6 pad_maximum_fusion
  251.6 2.6 copy.31
  254.2 0.0 reduce-scatter.4.cloned.1.call-update
  254.2 68.9 %all-to-all-done.2 = bf16[64,18,1024]{2,1,0:T(8,128)(2,1)} async-done(((bf16[64,18,1024]{2,1,0:T(8,128)(2,1)}), bf16[64,18,1024]{2,1,0:T(8,128)(2,1)}, u32[]{:S(2)}, u32[]{:S(2)}) %all-to-all-start.2) | async-done | bytes 2359328 | tf_op jit(solution)/shard_map/all_to_all | solution.py:102
  323.2 2.9 reshape.103
  326.1 5.4 %gather_fusion = bf16[1024,1024]{1,0:T(8,128)(2,1)} fusion(bf16[1152,1024]{1,0:T(8,128)(2,1)S(1)} %reshape.103, s32[1024]{0:T(1024)S(1)} %broadcast_clamp_fusion), kind=kCustom, calls=%fused_computation | custom fusion | bytes 4198400 | tf_op jit(solution)/shard_map/gather | solution.py:109
  331.5 3.7 %bitcast_reduce_fusion = bf16[128,1024]{1,0:T(8,128)(2,1)} fusion(bf16[1024,1024]{1,0:T(8,128)(2,1)} %gather_fusion), kind=kLoop, calls=%fused_computation.8 | loop fusion | flops 917504 | bytes 2359296 | tf_op jit(solution)/shard_map/reduce_sum | solution.py:112
  335.2 1.2 copy.32
  336.4 0.7 slice_bitcast_fusion
  337.1 0.8 copy.30
  337.9 0.8 copy.29
  (24 shorter events, 0.1 us)
Async XLA Ops:
  7.2 2.8 copy-start
  18.4 11.8 %copy-start.7 = (f32[128,8]{0,1:T(8,128)S(1)}, f32[128,8]{0,1:T(8,128)}, u32[]{:S(2)}) copy-start(f32[128,8]{0,1:T(8,128)} %param.9) | copy-start | bytes 12292
  18.4 85.3 %all-to-all-start.1 = ((bf16[64,18,1024]{2,1,0:T(8,128)(2,1)}), bf16[64,18,1024]{2,1,0:T(8,128)(2,1)S(1)}, u32[]{:S(2)}, u32[]{:S(2)}) async-start(bf16[64,18,1024]{2,1,0:T(8,128)(2,1)} %reshape.100), calls=%async_computation.1 | async-start | bytes 6291456 | tf_op jit(solution)/shard_map/all_to_all | solution.py:96
  44.2 78.4 %copy-start.5 = (bf16[1,128,384]{2,1,0:T(8,128)(2,1)S(1)}, bf16[1,128,384]{2,1,0:T(8,128)(2,1)}, u32[]{:S(2)}) copy-start(bf16[1,128,384]{2,1,0:T(8,128)(2,1)} %param.12) | copy-start | bytes 294916
  103.6 103.6 %all-to-all-start = ((bf16[64,18,1024]{2,1,0:T(8,128)(2,1)}), bf16[64,18,1024]{2,1,0:T(8,128)(2,1)}, u32[]{:S(2)}, u32[]{:S(2)}) async-start(bf16[64,18,1024]{2,1,0:T(8,128)(2,1)} %reshape.97), calls=%async_computation | async-start | bytes 6291456 | tf_op jit(solution)/shard_map/all_to_all | solution.py:97
  109.9 61.8 %collective-permute-start.1 = (bf16[1,128,384]{2,1,0:T(8,128)(2,1)}, bf16[1,128,384]{2,1,0:T(8,128)(2,1)}, u32[]{:S(2)}, u32[]{:S(2)}) collective-permute-start(bf16[1,128,384]{2,1,0:T(8,128)(2,1)} %param.11), channel_id=1, source_target_pairs={{0,448},{64,0},{128,64},{192,128},{256,192},{320,256},{384,320},{4... | collective-permute-start | bytes 294920 | tf_op jit(solution)/shard_map/ppermute | solution.py:23
  120.6 54.9 %collective-permute-start = (bf16[1,128,384]{2,1,0:T(8,128)(2,1)}, bf16[1,128,384]{2,1,0:T(8,128)(2,1)}, u32[]{:S(2)}, u32[]{:S(2)}) collective-permute-start(bf16[1,128,384]{2,1,0:T(8,128)(2,1)} %param.11), channel_id=1, source_target_pairs={{0,64},{64,128},{128,192},{192,256},{256,320},{320,384},{384,448},... | collective-permute-start | bytes 294920 | tf_op jit(solution)/shard_map/ppermute | solution.py:18
  122.5 48.5 %copy-start.6 = (bf16[1,128,384]{2,1,0:T(8,128)(2,1)S(1)}, bf16[1,128,384]{2,1,0:T(8,128)(2,1)}, u32[]{:S(2)}) copy-start(bf16[1,128,384]{2,1,0:T(8,128)(2,1)} %param.11) | copy-start | bytes 294916
  171.7 8.8 %collective-permute-start.3 = (bf16[1,128,384]{2,1,0:T(8,128)(2,1)}, bf16[1,128,384]{2,1,0:T(8,128)(2,1)S(1)}, u32[]{:S(2)}, u32[]{:S(2)}) collective-permute-start(bf16[1,128,384]{2,1,0:T(8,128)(2,1)} %collective-permute-done.1), channel_id=1, source_target_pairs={{0,448},{64,0},{128,64},{192,128},{256,192},{320,256},{384,320},{4... | collective-permute-start | bytes 294920 | tf_op jit(solution)/shard_map/ppermute | solution.py:23
  175.5 9.6 %collective-permute-start.2 = (bf16[1,128,384]{2,1,0:T(8,128)(2,1)}, bf16[1,128,384]{2,1,0:T(8,128)(2,1)S(1)}, u32[]{:S(2)}, u32[]{:S(2)}) collective-permute-start(bf16[1,128,384]{2,1,0:T(8,128)(2,1)} %collective-permute-done), channel_id=1, source_target_pairs={{0,64},{64,128},{128,192},{192,256},{256,320},{320,384},{384,448},... | collective-permute-start | bytes 294920 | tf_op jit(solution)/shard_map/ppermute | solution.py:18
  180.5 13.9 %collective-permute-start.5 = (bf16[1,128,384]{2,1,0:T(8,128)(2,1)S(1)}, bf16[1,128,384]{2,1,0:T(8,128)(2,1)S(1)}, u32[]{:S(2)}, u32[]{:S(2)}) collective-permute-start(bf16[1,128,384]{2,1,0:T(8,128)(2,1)S(1)} %collective-permute-done.3), channel_id=1, source_target_pairs={{0,448},{64,0},{128,64},{192,128},{256,192},{320,256},{384,320},{4... | collective-permute-start | bytes 294920 | tf_op jit(solution)/shard_map/ppermute | solution.py:23
  185.1 6.6 %collective-permute-start.4 = (bf16[1,128,384]{2,1,0:T(8,128)(2,1)S(1)}, bf16[1,128,384]{2,1,0:T(8,128)(2,1)S(1)}, u32[]{:S(2)}, u32[]{:S(2)}) collective-permute-start(bf16[1,128,384]{2,1,0:T(8,128)(2,1)S(1)} %collective-permute-done.2), channel_id=1, source_target_pairs={{0,64},{64,128},{128,192},{192,256},{256,320},{320,384},{384,448},... | collective-permute-start | bytes 294920 | tf_op jit(solution)/shard_map/ppermute | solution.py:18
  191.7 6.6 %collective-permute-start.6 = (bf16[1,128,384]{2,1,0:T(8,128)(2,1)S(1)}, bf16[1,128,384]{2,1,0:T(8,128)(2,1)S(1)}, u32[]{:S(2)}, u32[]{:S(2)}) collective-permute-start(bf16[1,128,384]{2,1,0:T(8,128)(2,1)S(1)} %collective-permute-done.4), channel_id=1, source_target_pairs={{0,64},{64,128},{128,192},{192,256},{256,320},{320,384},{384,448},... | collective-permute-start | bytes 294920 | tf_op jit(solution)/shard_map/ppermute | solution.py:18
  210.1 1.4 copy-start.2
  211.6 3.4 copy-start.4
  211.6 3.4 copy-start.8
  215.0 3.4 copy-start.1
  218.4 3.3 copy-start.3
  227.4 95.8 %all-to-all-start.2 = ((bf16[64,18,1024]{2,1,0:T(8,128)(2,1)}), bf16[64,18,1024]{2,1,0:T(8,128)(2,1)}, u32[]{:S(2)}, u32[]{:S(2)}) async-start(bf16[64,18,1024]{2,1,0:T(8,128)(2,1)} %reshape.102), calls=%async_computation.2 | async-start | bytes 6291456 | tf_op jit(solution)/shard_map/all_to_all | solution.py:102
  249.7 85.5 %reduce-scatter.4.cloned.1.call-start = ((), (), s32[]{:S(2)}) async-start(), calls=%async_computation.4 | async-start | bytes 2654208
Sparse Core Ops, SparseCore 0:
  254.3 39.2 reduce-scatter.3
